TPU v7x, 32 devices: a whole 2x2x4 slice. The times are simulated.
32 devices in a mesh: blk: 8 (over y, x, core), lines: 4 (over z).
Axes of the slice: x: 2, y: 2, z: 4, core: 2. Of those that a mesh axis runs over, the one named last changes fastest.
Arguments:
- velocity: float32 [3, 12288, 1024], P(None, 'lines', 'blk'), may hold values from -6 to 6
- metric: float32 [1024], P('blk'), may hold values from 0.5 to 2
Outputs:
- derivs: float32 [3, 12288, 1024], P(None, 'lines', 'blk')
- profile: float32 [1024], P('blk')
All inputs are finite; a program needn't handle non-finite values.
Results may differ from a plain program's by a relative error of at most 0.00007.
Values sent between devices are 32-bit elements; how exact they have to be, the bound alone decides.
No kernel may reach another device: no remote copies, remote signals or barrier semaphores. Data moves between devices by JAX's collectives and lax.ppermute only.
A program may use at most 128 MiB of HBM per device.

v0:
```python
import jax
import jax.numpy as jnp
from jax import lax
from jax.sharding import PartitionSpec as P

ALPHA = 1.0 / 3.0
COEF_A = 7.0 / 9.0
COEF_B = 1.0 / 36.0


def block_inverse(width):
    counter = jnp.arange(width, dtype=jnp.int32) + 1
    product = counter[:, None] * counter[None, :] % (2 * (width + 1))
    angles = jnp.pi / (width + 1.0)
    sines = jnp.sqrt(2.0 / (width + 1.0)) * jnp.sin(angles * product.astype(jnp.float32))
    eigen = 1.0 + 2.0 * ALPHA * jnp.cos(angles * counter.astype(jnp.float32))
    return jnp.dot(sines / eigen[None, :], sines, precision=lax.Precision.HIGHEST)


def solve_rows(source, inverse):
    shape = source.shape
    flat = jnp.dot(source.reshape(-1, shape[-1]), inverse, precision=lax.Precision.HIGHEST)
    return flat.reshape(shape)


def interface(first_own, last_own, last_left, first_right, couple):
    factor = 1.0 / (1.0 - couple * couple)
    last_prev = (last_left - couple * first_own) * factor
    last_here = (last_own - couple * first_right) * factor
    first_next = first_right - couple * last_here
    return (last_prev, first_next)


def correct(partial_value, inverse, last_prev, first_next):
    width = inverse.shape[0]
    return partial_value - ALPHA * (
        last_prev[..., None] * inverse[:, 0] + first_next[..., None] * inverse[:, width - 1]
    )


def local(velocity, metric):
    width = velocity.shape[2]
    inverse = block_inverse(width)
    couple = ALPHA * inverse[0, 0]
    lines_block = lax.all_to_all(velocity, "blk", split_axis=1, concat_axis=2, tiled=True)
    count = lines_block.shape[-1]
    source = COEF_A * (jnp.roll(lines_block, -1, -1) - jnp.roll(lines_block, 1, -1)) + COEF_B * (
        jnp.roll(lines_block, -2, -1) - jnp.roll(lines_block, 2, -1)
    )
    blocks = source.reshape(lines_block.shape[0], lines_block.shape[1], count // width, width)
    partial_value = solve_rows(blocks, inverse)
    first_own = partial_value[..., 0]
    last_own = partial_value[..., width - 1]
    last_prev, first_next = interface(
        first_own, last_own, jnp.roll(last_own, 1, 2), jnp.roll(first_own, -1, 2), couple
    )
    whole = correct(partial_value, inverse, last_prev, first_next).reshape(lines_block.shape)
    solved = lax.all_to_all(whole, "blk", split_axis=2, concat_axis=1, tiled=True)
    derivs = solved * metric
    squares = jnp.sum(derivs * derivs, axis=(0, 1))
    total = lax.psum(squares, "lines")
    profile = total / (velocity.shape[1] * lax.axis_size("lines"))
    return (derivs, profile)


def solution(mesh):
    in_specs = (P(None, "lines", "blk"), P("blk"))
    out_specs = (P(None, "lines", "blk"), P("blk"))
    return jax.shard_map(local, mesh=mesh, in_specs=in_specs, out_specs=out_specs, check_vma=False)
```

profile of v0, /device:TPU:0, one launch (start us, length us, event | category | flops | bytes accessed | tf_op | source)
XLA Modules:
  0.0 224.0 jit_solution(313442755634897913)
XLA Ops:
  0.6 8.7 %copy.19 = f32[3,3072,128]{2,0,1:T(4,128)} copy(f32[3,3072,128]{2,1,0:T(8,128)} %param.2) | data formatting | bytes 9437184 | tf_op args[0]
  9.3 5.2 %all-to-all-start = ((f32[3,3072,128]{2,0,1:T(4,128)}), f32[3,3072,128]{2,0,1:T(4,128)}, u32[]{:S(2)}, u32[]{:S(2)}) async-start(f32[3,3072,128]{2,0,1:T(4,128)} %copy.19), calls=%async_computation | async-start | bytes 12582912 | tf_op jit(solution)/shard_map/all_to_all | solution.py:45
  14.6 0.9 fusion.3
  15.4 0.5 slice.91
  17.9 68.4 %all-to-all-done = f32[3,3072,128]{2,0,1:T(4,128)} async-done(((f32[3,3072,128]{2,0,1:T(4,128)}), f32[3,3072,128]{2,0,1:T(4,128)}, u32[]{:S(2)}, u32[]{:S(2)}) %all-to-all-start) | async-done | bytes 4718624 | tf_op jit(solution)/shard_map/all_to_all | solution.py:45
  86.3 5.3 %copy.20 = f32[3,3072,128]{2,1,0:T(8,128)} copy(f32[3,3072,128]{2,0,1:T(4,128)} %all-to-all-done) | data formatting | bytes 9437184 | tf_op jit(solution)/shard_map/all_to_all | solution.py:45
  91.6 6.1 %copy.21 = f32[3,384,8,128]{1,3,2,0:T(8,128)} copy(f32[3,384,8,128]{3,1,2,0:T(8,128)} %bitcast.50) | data formatting | bytes 9437184 | tf_op jit(solution)/shard_map/all_to_all | solution.py:45
  97.7 0.0 copy-start
  97.7 4.5 %fusion.33 = (f32[3,384,1023]{1,2,0:T(8,128)S(1)}, f32[3,384,1023]{1,2,0:T(8,128)S(1)}) fusion(f32[3,384,1024]{1,2,0:T(8,128)} %bitcast.42), kind=kLoop, calls=%fused_computation.53 | loop fusion | bytes 18855936 | tf_op jit(solution)/shard_map/jit(_roll_static)/slice | solution.py:47
  102.2 0.6 copy-done
  102.8 2.8 %fusion.31 = (f32[3,384,1022]{1,2,0:T(8,128)S(1)}, f32[3,384,1022]{1,2,0:T(8,128)}) fusion(f32[3,384,1024]{1,2,0:T(8,128)S(1)} %bitcast.43), kind=kLoop, calls=%fused_computation.51 | loop fusion | bytes 18837504 | tf_op jit(solution)/shard_map/jit(_roll_static)/slice | solution.py:48
  105.6 6.7 %fusion.1 = f32[3,384,1024]{1,2,0:T(8,128)S(1)} fusion(f32[3,384,1]{1,2,0:T(1,128)S(1)} %get-tuple-element.9, f32[3,384,1023]{1,2,0:T(8,128)S(1)} %get-tuple-element.11, f32[3,384,1023]{1,2,0:T(8,128)S(1)} %get-tuple-element.10, f32[3,384,1]{1,2,0:T(1,128)S(1)} %get-tuple-element.8, f32[3,384,2]{1,2,0:T(2,128)S(1)} %get-tuple-element.5, ...), kind=kLoop, calls=%fused_computation.3 | loop fusion | flops 10616832 | bytes 23592960 | tf_op jit(solution)/shard_map/add | solution.py:47
  112.3 4.7 %fusion.10 = f32[3,384,8,128]{1,3,2,0:T(8,128)S(1)} fusion(f32[3,384,8,128]{1,3,2,0:T(8,128)S(1)} %bitcast.48, f32[128,128]{0,1:T(8,128)S(1)} %fusion.3), kind=kOutput, calls=%fused_computation.15 | convolution fusion | flops 1811939328 | bytes 9502720 | tf_op jit(solution)/shard_map/dot_general | solution.py:22
  117.1 0.1 fusion.29
  117.3 1.0 multiply_subtract_fusion
  118.3 3.2 %copy.26 = f32[3,384,1024]{1,0,2:T(4,128)S(1)} copy(f32[3,384,1024]{1,2,0:T(8,128)S(1)} %bitcast.49) | data formatting | bytes 9437184 | tf_op jit(solution)/shard_map/reshape | solution.py:57
  121.5 74.9 %all_to_all.36 = f32[3,384,1024]{1,0,2:T(4,128)} all-to-all(f32[3,384,1024]{1,0,2:T(4,128)S(1)} %copy.26), channel_id=1, replica_groups=mesh['blk'=8,'lines'=4] {'blk'}, dimensions={2} | all-to-all | bytes 9437184 | tf_op jit(solution)/shard_map/all_to_all | solution.py:58
  196.4 0.0 copy-start.2
  196.4 6.9 %copy.27 = f32[3,8,384,128]{3,2,1,0:T(8,128)} copy(f32[3,8,384,128]{2,0,3,1:T(4,128)} %bitcast.46) | data formatting | bytes 9437184 | tf_op jit(solution)/shard_map/all_to_all | solution.py:58
  203.3 0.0 copy-done.2
  203.3 0.0 copy-start.1
  203.3 4.9 %multiply_reduce_fusion = f32[128]{0:T(128)S(1)} fusion(f32[3,8,384,128]{2,0,3,1:T(4,128)} %bitcast.47, f32[128]{0:T(128)S(1)} %copy-done.2), kind=kLoop, calls=%fused_computation | loop fusion | flops 3538816 | bytes 4719616 | tf_op jit(solution)/shard_map/reduce_sum | solution.py:60
  208.3 0.0 copy-done.1
  208.3 2.5 %bitcast_multiply_fusion = f32[3,3072,128]{2,1,0:T(8,128)} fusion(f32[3,8,384,128]{3,2,1,0:T(8,128)S(1)} %copy-done.1, f32[128]{0:T(128)S(1)} %copy-done.2), kind=kLoop, calls=%fused_computation.6 | loop fusion | flops 1179648 | bytes 9437696 | tf_op jit(solution)/shard_map/mul | solution.py:59
  210.8 12.7 %psum.7 = f32[128]{0:T(128)S(1)} all-reduce(f32[128]{0:T(128)S(1)} %multiply_reduce_fusion), channel_id=1, replica_groups=mesh['blk'=8,'lines'=4] {'lines'}, use_global_device_ids=true, to_apply=%region_1.2 | all-reduce | flops 128 | bytes 1024 | tf_op jit(solution)/shard_map/psum | solution.py:61
  223.5 0.5 broadcast_multiply_fusion
  (12 shorter events, 0.1 us)
Async XLA Ops:
  9.3 77.0 %all-to-all-start = ((f32[3,3072,128]{2,0,1:T(4,128)}), f32[3,3072,128]{2,0,1:T(4,128)}, u32[]{:S(2)}, u32[]{:S(2)}) async-start(f32[3,3072,128]{2,0,1:T(4,128)} %copy.19), calls=%async_computation | async-start | bytes 12582912 | tf_op jit(solution)/shard_map/all_to_all | solution.py:45
  97.7 5.1 %copy-start = (f32[3,384,8,128]{1,3,2,0:T(8,128)S(1)}, f32[3,384,8,128]{1,3,2,0:T(8,128)}, u32[]{:S(2)}) copy-start(f32[3,384,8,128]{1,3,2,0:T(8,128)} %copy.21) | copy-start | bytes 14155780
  196.4 6.9 %copy-start.2 = (f32[128]{0:T(128)S(1)}, f32[128]{0:T(128)}, u32[]{:S(2)}) copy-start(f32[128]{0:T(128)} %param.3) | copy-start | bytes 1540
  203.3 5.0 %copy-start.1 = (f32[3,8,384,128]{3,2,1,0:T(8,128)S(1)}, f32[3,8,384,128]{3,2,1,0:T(8,128)}, u32[]{:S(2)}) copy-start(f32[3,8,384,128]{3,2,1,0:T(8,128)} %copy.27) | copy-start | bytes 14155780
where the time goes:
time: 225 us; the launch traced here: 224 us
  blocking collectives  87.6 us (39%)
  waiting for transfers between devices  68.4 us (30%)
  local copies, waits for them, and re-layouts  38.7 us (17%)
  other arithmetic  15.8 us (7%)
  matrix products  5.58 us (2%)
  starting transfers between devices  5.17 us (2%)
  between operations  2.74 us (1%)
    all_to_all x1, blocking collectives, local(): lax.all_to_all(whole, 'blk', split_axis=2, concat_axis=1, tiled=True)  74.9 us
    all_to_all x1, waiting for transfers between devices, local(): lax.all_to_all(velocity, 'blk', split_axis=1, concat_axis=2, tiled=True)  68.4 us
    psum x1, blocking collectives, local(): total = lax.psum(squares, 'lines')  12.7 us
    all_to_all x2, local copies, waits for them, and re-layouts, local(): lax.all_to_all(velocity, 'blk', split_axis=1, concat_axis=2, tiled=True)  11.3 us
    unnamed x8, local copies, waits for them, and re-layouts  9.3 us
    all_to_all x1, local copies, waits for them, and re-layouts, local(): lax.all_to_all(whole, 'blk', split_axis=2, concat_axis=1, tiled=True)  6.91 us
    add x1, other arithmetic, local(): COEF_A * (jnp.roll(lines_block, -1, -1) - jnp.roll(lines_block, 1, -1))  6.72 us
    all_to_all x1, starting transfers between devices, local(): lax.all_to_all(velocity, 'blk', split_axis=1, concat_axis=2, tiled=True)  5.17 us
  transfers between devices with their start and end apart: 1, of which 1 were waited for; matrix products, arithmetic and copies ran while one was open for 1% of the time, Pallas kernels for 0%

commit v1 on v0

--- a/solution.py
+++ b/solution.py
@@ -42,7 +42,27 @@
     width = velocity.shape[2]
     inverse = block_inverse(width)
     couple = ALPHA * inverse[0, 0]
-    lines_block = lax.all_to_all(velocity, "blk", split_axis=1, concat_axis=2, tiled=True)
+
+    def words_note(chunk, lane_axis):
+        odd, parts_out = (lax.axis_size(lane_axis), lax.axis_index(lane_axis))
+        block_next = chunk.shape[1] // odd
+        lower = list(chunk.shape)
+        lower[1] = block_next
+        seen_now = lower[2]
+        lower[2] = seen_now * odd
+        row_out = jnp.zeros(lower, chunk.dtype)
+        for p in range(odd):
+            m_next = lax.dynamic_slice_in_dim(
+                chunk, (parts_out ^ p) * block_next, block_next, axis=1
+            )
+            if p:
+                m_next = lax.ppermute(m_next, lane_axis, [(u, u ^ p) for u in range(odd)])
+            row_out = lax.dynamic_update_slice_in_dim(
+                row_out, m_next, (parts_out ^ p) * seen_now, axis=2
+            )
+        return row_out
+
+    lines_block = words_note(velocity, "blk")
     count = lines_block.shape[-1]
     source = COEF_A * (jnp.roll(lines_block, -1, -1) - jnp.roll(lines_block, 1, -1)) + COEF_B * (
         jnp.roll(lines_block, -2, -1) - jnp.roll(lines_block, 2, -1)

time: 225 us -> 189 us (0.84)
  waiting for transfers between devices: 68.4 us -> 37.4 us
  local copies, waits for them, and re-layouts: 38.7 us -> 30.1 us
  starting transfers between devices: 5.17 us -> 9.35 us
    all_to_all x1 -> x0, waiting for transfers between devices: 68.4 us -> none  [local(): lax.all_to_all(velocity, 'blk', split_axis=1, concat_axis=2, tiled=True)]
    ppermute x0 -> x7, waiting for transfers between devices: none -> 37.4 us  [words_note(): m_next = lax.ppermute(m_next, lane_axis, [(u, u ^ p) for u in range(odd)])]
    all_to_all x2 -> x0, local copies, waits for them, and re-layouts: 11.3 us -> none  [local(): lax.all_to_all(velocity, 'blk', split_axis=1, concat_axis=2, tiled=True)]
    ppermute x0 -> x7, starting transfers between devices: none -> 9.35 us  [words_note(): m_next = lax.ppermute(m_next, lane_axis, [(u, u ^ p) for u in range(odd)])]
    all_to_all x1 -> x0, starting transfers between devices: 5.17 us -> none  [local(): lax.all_to_all(velocity, 'blk', split_axis=1, concat_axis=2, tiled=True)]
    dynamic_update_slice x0 -> x8, local copies, waits for them, and re-layouts: none -> 4.6 us  [words_note(): lax.dynamic_update_slice_in_dim(row_out, m_next, (parts_out ^ p) * seen_n...]
    slice x2, local copies, waits for them, and re-layouts: 4.52 us -> 0.63 us  [local(): jnp.roll(lines_block, 1, -1)]
    dynamic_slice x0 -> x1, local copies, waits for them, and re-layouts: none -> 3.67 us  [words_note(): lax.dynamic_slice_in_dim(chunk, (parts_out ^ p) * block_next, block_next,...]
  transfers between devices with their start and end apart: 1 -> 7, of which waited for: 1 -> 3; matrix products, arithmetic and copies ran while one was open for 1% -> 6% of each run, Pallas kernels for 0% -> 0%
where the time goes in v1:
time: 189 us
  blocking collectives  87.4 us (46%)
  waiting for transfers between devices  37.4 us (20%)
  local copies, waits for them, and re-layouts  30.1 us (16%)
  other arithmetic  15.8 us (8%)
  starting transfers between devices  9.35 us (5%)
  matrix products  5.58 us (3%)
  between operations  3 us (2%)
    all_to_all x1, blocking collectives, local(): lax.all_to_all(whole, 'blk', split_axis=2, concat_axis=1, tiled=True)  75.4 us
    ppermute x7, waiting for transfers between devices, words_note(): m_next = lax.ppermute(m_next, lane_axis, [(u, u ^ p) for u in range(odd)])  37.4 us
    psum x1, blocking collectives, local(): total = lax.psum(squares, 'lines')  11.9 us
    ppermute x7, starting transfers between devices, words_note(): m_next = lax.ppermute(m_next, lane_axis, [(u, u ^ p) for u in range(odd)])  9.35 us
    unnamed x17, local copies, waits for them, and re-layouts  7.34 us
    all_to_all x1, local copies, waits for them, and re-layouts, local(): lax.all_to_all(whole, 'blk', split_axis=2, concat_axis=1, tiled=True)  6.91 us
    add x1, other arithmetic, local(): COEF_A * (jnp.roll(lines_block, -1, -1) - jnp.roll(lines_block, 1, -1))  6.72 us
    reduce_sum x1, other arithmetic, local(): squares = jnp.sum(derivs * derivs, axis=(0, 1))  4.95 us
  transfers between devices with their start and end apart: 7, of which 3 were waited for; matrix products, arithmetic and copies ran while one was open for 6% of the time, Pallas kernels for 0%

profile of v1, /device:TPU:0, one launch (start us, length us, event | category | flops | bytes accessed | tf_op | source)
XLA Modules:
  0.0 188.7 jit_solution(17824313694933770111)
XLA Ops:
  0.7 3.7 %constant_dynamic-slice_fusion = (f32[3,384,128]{2,1,0:T(8,128)S(1)}, f32[3,384,128]{2,1,0:T(8,128)S(1)}, f32[3,384,128]{2,1,0:T(8,128)S(1)}, f32[3,384,128]{2,1...) fusion(f32[3,3072,128]{2,1,0:T(8,128)} %param.2, ...), kind=kLoop, calls=%fused_computation.42 | loop fusion | bytes 9437216 | tf_op jit(solution)/shard_map/dynamic_slice | solution.py:55
  4.4 2.1 %copy.39 = f32[3,384,128]{1,2,0:T(8,128)} copy(f32[3,384,128]{2,1,0:T(8,128)} %get-tuple-element.18) | data formatting | bytes 1179648
  6.5 0.5 collective-permute-start
  6.9 2.1 %copy.40 = f32[3,384,128]{1,2,0:T(8,128)} copy(f32[3,384,128]{2,1,0:T(8,128)} %get-tuple-element.17) | data formatting | bytes 1179648
  9.1 2.5 %collective-permute-start.1 = (f32[3,384,128]{1,2,0:T(8,128)}, f32[3,384,128]{1,2,0:T(8,128)}, u32[]{:S(2)}, u32[]{:S(2)}) collective-permute-start(f32[3,384,128]{1,2,0:T(8,128)} %copy.40), channel_id=1, source_target_pairs={{0,8},{4,12},{8,0},{12,4},{16,24},{20,28},{24,16},{28,20},{1,9},{5... | collective-permute-start | bytes 1769480 | tf_op jit(solution)/shard_map/ppermute | solution.py:59
  11.5 1.0 copy.41
  12.6 0.1 collective-permute-start.2
  12.7 1.0 copy.42
  13.8 1.8 collective-permute-start.3
  15.5 0.2 copy.43
  15.8 0.1 collective-permute-start.4
  15.9 0.9 fusion.3
  16.7 0.0 copy-start.1
  16.8 0.5 slice.91
  17.3 0.1 copy-done.1
  17.4 0.2 copy.38
  17.6 0.2 copy.44
  17.8 0.2 copy.45
  20.1 0.3 broadcast_in_dim.2
  20.5 0.0 collective-permute-done
  20.5 2.6 %collective-permute-start.5 = (f32[3,384,128]{1,2,0:T(8,128)S(1)}, f32[3,384,128]{1,2,0:T(8,128)S(1)}, u32[]{:S(2)}, u32[]{:S(2)}) collective-permute-start(f32[3,384,128]{1,2,0:T(8,128)S(1)} %copy.44), channel_id=1, source_target_pairs={{0,24},{4,28},{8,16},{12,20},{16,8},{20,12},{24,0},{28,4},{1,25},{... | collective-permute-start | bytes 1769480 | tf_op jit(solution)/shard_map/ppermute | solution.py:59
  23.1 1.1 constant_dynamic-update-slice_fusion.6
  24.2 1.8 collective-permute-done.1
  26.0 1.8 collective-permute-start.6
  27.9 1.1 constant_dynamic-update-slice_fusion.5
  29.0 9.3 %collective-permute-done.2 = f32[3,384,128]{1,2,0:T(8,128)} collective-permute-done((f32[3,384,128]{1,2,0:T(8,128)}, f32[3,384,128]{1,2,0:T(8,128)}, u32[]{:S(2)}, u32[]{:S(2)}) %collective-permute-start.2) | collective-permute-done | bytes 589856 | tf_op jit(solution)/shard_map/ppermute | solution.py:59
  38.3 1.1 constant_dynamic-update-slice_fusion.4
  39.4 0.0 collective-permute-done.3
  39.4 1.1 constant_dynamic-update-slice_fusion.3
  40.5 26.3 %collective-permute-done.4 = f32[3,384,128]{1,2,0:T(8,128)S(1)} collective-permute-done((f32[3,384,128]{1,2,0:T(8,128)S(1)}, f32[3,384,128]{1,2,0:T(8,128)S(1)}, u32[]{:S(2)}, u32[]{:S(2)}) %collective-permute-start.4) | collective-permute-done | bytes 589856 | tf_op jit(solution)/shard_map/ppermute | solution.py:59
  66.9 0.0 collective-permute-done.5
  66.9 0.0 collective-permute-done.6
  67.0 0.6 fusion.33
  67.6 2.8 %fusion.31 = (f32[3,384,1022]{1,2,0:T(8,128)S(1)}, f32[3,384,1022]{1,2,0:T(8,128)}) fusion(f32[3,384,1024]{1,2,0:T(8,128)S(1)} %constant_dynamic-update-slice_fusion), kind=kLoop, calls=%fused_computation.67 | loop fusion | bytes 18837504 | tf_op jit(solution)/shard_map/jit(_roll_static)/slice | solution.py:68
  70.5 0.0 copy-start.2
  70.5 6.7 %fusion.1 = f32[3,384,1024]{1,2,0:T(8,128)S(1)} fusion(f32[3,384,1]{1,2,0:T(1,128)S(1)} %get-tuple-element.9, f32[3,384,1023]{1,2,0:T(8,128)S(1)} %get-tuple-element.11, f32[3,384,1023]{1,2,0:T(8,128)S(1)} %get-tuple-element.10, f32[3,384,1]{1,2,0:T(1,128)S(1)} %get-tuple-element.8, f32[3,384,2]{1,2,0:T(2,128)S(1)} %get-tuple-element.5, ...), kind=kLoop, calls=%fused_computation.3 | loop fusion | flops 10616832 | bytes 23592960 | tf_op jit(solution)/shard_map/add | solution.py:67
  77.2 0.0 copy-done.2
  77.2 4.7 %fusion.10 = f32[3,384,8,128]{1,3,2,0:T(8,128)S(1)} fusion(f32[3,384,8,128]{1,3,2,0:T(8,128)S(1)} %bitcast.40, f32[128,128]{0,1:T(8,128)S(1)} %copy-done.2), kind=kOutput, calls=%fused_computation.15 | convolution fusion | flops 1811939328 | bytes 9502720 | tf_op jit(solution)/shard_map/dot_general | solution.py:22
  82.0 0.1 fusion.29
  82.1 1.0 multiply_subtract_fusion
  83.2 3.2 %copy.33 = f32[3,384,1024]{1,0,2:T(4,128)S(1)} copy(f32[3,384,1024]{1,2,0:T(8,128)S(1)} %bitcast.41) | data formatting | bytes 9437184 | tf_op jit(solution)/shard_map/reshape | solution.py:77
  86.4 75.4 %all_to_all.18 = f32[3,384,1024]{1,0,2:T(4,128)} all-to-all(f32[3,384,1024]{1,0,2:T(4,128)S(1)} %copy.33), channel_id=1, replica_groups=mesh['blk'=8,'lines'=4] {'blk'}, dimensions={2} | all-to-all | bytes 9437184 | tf_op jit(solution)/shard_map/all_to_all | solution.py:78
  161.8 0.0 copy-start.3
  161.8 6.9 %copy.34 = f32[3,8,384,128]{3,2,1,0:T(8,128)} copy(f32[3,8,384,128]{2,0,3,1:T(4,128)} %bitcast.38) | data formatting | bytes 9437184 | tf_op jit(solution)/shard_map/all_to_all | solution.py:78
  168.8 0.0 copy-done.3
  168.8 0.0 copy-start
  168.8 4.9 %multiply_reduce_fusion = f32[128]{0:T(128)S(1)} fusion(f32[3,8,384,128]{2,0,3,1:T(4,128)} %bitcast.39, f32[128]{0:T(128)S(1)} %copy-done.3), kind=kLoop, calls=%fused_computation | loop fusion | flops 3538816 | bytes 4719616 | tf_op jit(solution)/shard_map/reduce_sum | solution.py:80
  173.7 0.0 copy-done
  173.7 2.5 %bitcast_multiply_fusion = f32[3,3072,128]{2,1,0:T(8,128)} fusion(f32[3,8,384,128]{3,2,1,0:T(8,128)S(1)} %copy-done, f32[128]{0:T(128)S(1)} %copy-done.3), kind=kLoop, calls=%fused_computation.6 | loop fusion | flops 1179648 | bytes 9437696 | tf_op jit(solution)/shard_map/mul | solution.py:79
  176.2 11.9 %psum.7 = f32[128]{0:T(128)S(1)} all-reduce(f32[128]{0:T(128)S(1)} %multiply_reduce_fusion), channel_id=1, replica_groups=mesh['blk'=8,'lines'=4] {'lines'}, use_global_device_ids=true, to_apply=%region_1.2 | all-reduce | flops 128 | bytes 1024 | tf_op jit(solution)/shard_map/psum | solution.py:81
  188.1 0.5 broadcast_multiply_fusion
  (16 shorter events, 0.3 us)
Async XLA Ops:
  6.5 14.0 %collective-permute-start = (f32[3,384,128]{1,2,0:T(8,128)}, f32[3,384,128]{1,2,0:T(8,128)}, u32[]{:S(2)}, u32[]{:S(2)}) collective-permute-start(f32[3,384,128]{1,2,0:T(8,128)} %copy.39), channel_id=1, source_target_pairs={{0,4},{4,0},{8,12},{12,8},{16,20},{20,16},{24,28},{28,24},{1,5},{5... | collective-permute-start | bytes 1769480 | tf_op jit(solution)/shard_map/ppermute | solution.py:59
  9.1 17.0 %collective-permute-start.1 = (f32[3,384,128]{1,2,0:T(8,128)}, f32[3,384,128]{1,2,0:T(8,128)}, u32[]{:S(2)}, u32[]{:S(2)}) collective-permute-start(f32[3,384,128]{1,2,0:T(8,128)} %copy.40), channel_id=1, source_target_pairs={{0,8},{4,12},{8,0},{12,4},{16,24},{20,28},{24,16},{28,20},{1,9},{5... | collective-permute-start | bytes 1769480 | tf_op jit(solution)/shard_map/ppermute | solution.py:59
  12.6 25.7 %collective-permute-start.2 = (f32[3,384,128]{1,2,0:T(8,128)}, f32[3,384,128]{1,2,0:T(8,128)}, u32[]{:S(2)}, u32[]{:S(2)}) collective-permute-start(f32[3,384,128]{1,2,0:T(8,128)} %copy.41), channel_id=1, source_target_pairs={{0,12},{4,8},{8,4},{12,0},{16,28},{20,24},{24,20},{28,16},{1,13},{... | collective-permute-start | bytes 1769480 | tf_op jit(solution)/shard_map/ppermute | solution.py:59
  13.8 25.7 %collective-permute-start.3 = (f32[3,384,128]{1,2,0:T(8,128)}, f32[3,384,128]{1,2,0:T(8,128)}, u32[]{:S(2)}, u32[]{:S(2)}) collective-permute-start(f32[3,384,128]{1,2,0:T(8,128)} %copy.42), channel_id=1, source_target_pairs={{0,16},{4,20},{8,24},{12,28},{16,0},{20,4},{24,8},{28,12},{1,17},{... | collective-permute-start | bytes 1769480 | tf_op jit(solution)/shard_map/ppermute | solution.py:59
  15.8 51.1 %collective-permute-start.4 = (f32[3,384,128]{1,2,0:T(8,128)S(1)}, f32[3,384,128]{1,2,0:T(8,128)S(1)}, u32[]{:S(2)}, u32[]{:S(2)}) collective-permute-start(f32[3,384,128]{1,2,0:T(8,128)S(1)} %copy.43), channel_id=1, source_target_pairs={{0,20},{4,16},{8,28},{12,24},{16,4},{20,0},{24,12},{28,8},{1,21},{... | collective-permute-start | bytes 1769480 | tf_op jit(solution)/shard_map/ppermute | solution.py:59
  16.7 0.6 copy-start.1
  20.5 46.4 %collective-permute-start.5 = (f32[3,384,128]{1,2,0:T(8,128)S(1)}, f32[3,384,128]{1,2,0:T(8,128)S(1)}, u32[]{:S(2)}, u32[]{:S(2)}) collective-permute-start(f32[3,384,128]{1,2,0:T(8,128)S(1)} %copy.44), channel_id=1, source_target_pairs={{0,24},{4,28},{8,16},{12,20},{16,8},{20,12},{24,0},{28,4},{1,25},{... | collective-permute-start | bytes 1769480 | tf_op jit(solution)/shard_map/ppermute | solution.py:59
  26.0 40.9 %collective-permute-start.6 = (f32[3,384,128]{1,2,0:T(8,128)S(1)}, f32[3,384,128]{1,2,0:T(8,128)S(1)}, u32[]{:S(2)}, u32[]{:S(2)}) collective-permute-start(f32[3,384,128]{1,2,0:T(8,128)S(1)} %copy.45), channel_id=1, source_target_pairs={{0,28},{4,24},{8,20},{12,16},{16,12},{20,8},{24,4},{28,0},{1,29},{... | collective-permute-start | bytes 1769480 | tf_op jit(solution)/shard_map/ppermute | solution.py:59
  70.5 6.7 %copy-start.2 = (f32[128,128]{0,1:T(8,128)S(1)}, f32[128,128]{0,1:T(8,128)}, u32[]{:S(2)}) copy-start(f32[128,128]{0,1:T(8,128)} %copy-done.1) | copy-start | bytes 196612
  161.8 6.9 %copy-start.3 = (f32[128]{0:T(128)S(1)}, f32[128]{0:T(128)}, u32[]{:S(2)}) copy-start(f32[128]{0:T(128)} %param.3) | copy-start | bytes 1540
  168.8 5.0 %copy-start = (f32[3,8,384,128]{3,2,1,0:T(8,128)S(1)}, f32[3,8,384,128]{3,2,1,0:T(8,128)}, u32[]{:S(2)}) copy-start(f32[3,8,384,128]{3,2,1,0:T(8,128)} %copy.34) | copy-start | bytes 14155780
